TPU v7x, 32 devices: a whole 2x2x4 slice. The times are simulated.
32 devices in a mesh: dp: 4 (over y, core), tensor: 8 (over z, x).
Axes of the slice: x: 2, y: 2, z: 4, core: 2. Of those that a mesh axis runs over, the one named last changes fastest.
Arguments:
- tokens: bfloat16 [512, 8192], P('dp', 'tensor'), may hold values from -6 to 6
- grad_out: bfloat16 [512, 8192], P('dp', 'tensor'), may hold values from -6 to 6
- packed_weight_blocks: float32 [2048, 128, 128], P(('dp', 'tensor')), may hold values from -4 to 4
- packed_first_moments: float32 [2048, 128, 128], P(('dp', 'tensor')), may hold values from -2 to 2
- packed_second_moments: float32 [2048, 128, 128], P(('dp', 'tensor')), may hold values from 0.05 to 1
- block_mask: int32 [2, 64, 128], P(None, None, 'tensor'), may hold values from 0 to 1, as said below
- last_step: int32 [2, 64, 128], P(None, None, 'tensor'), may hold values from 130 to 139
- regrown: int32 [2, 64, 128], P(None, None, 'tensor'), may hold values 0 or 1
- step_now: int32 [1], replicated, may hold values from 140 to 149
Outputs:
- input_grad: bfloat16 [512, 8192], P('dp', 'tensor')
- new_weights: float32 [2048, 128, 128], P(('dp', 'tensor'))
- new_first: float32 [2048, 128, 128], P(('dp', 'tensor'))
- new_second: float32 [2048, 128, 128], P(('dp', 'tensor'))
Inputs may be any that keep to these rules, and one draw needn't show every extreme that they name: `block_mask`: within one tensor shard's 16 block columns, both matrices together hold between 128 and 256 active blocks; some shard holds exactly 256.
All inputs are finite; a program needn't handle non-finite values. No bound on the sum of `regrown` on one device may be relied on, other than what follows from the above.
Results may differ from a plain program's by a relative error of at most 0.014.
Values may be sent and summed in bfloat16 or wider, within the bound.
A program may use at most 192 MiB of HBM per device.

v0:
```python
import functools
import math

import jax
import jax.numpy as jnp
from jax import lax
from jax.experimental import pallas as pl
from jax.experimental.pallas import tpu as pltpu
from jax.sharding import PartitionSpec as P

D = 8192


beta_one = 0.9
beta_two = 0.95
learn_rate = 0.05
decay_rate = 0.1
epsilon = 0.05


def silu_slope(values):
    sigmoid = jax.nn.sigmoid(values)
    return sigmoid * (1.0 + values * (1.0 - sigmoid))


def slot_table(mask_grid, regrown_grid, last_grid, slot_total):
    codes = lax.optimization_barrier((mask_grid + 2 * regrown_grid + 4 * last_grid).reshape(-1))
    flags = codes & 1
    numbered = jnp.cumsum(flags, dtype=jnp.int32) - 1
    block_total = flags.shape[0]
    wanted = jnp.where(flags == 1, numbered, -1)
    entries = jnp.arange(block_total, dtype=jnp.int32) + block_total * (codes >> 1)
    matches = wanted[None, :] == jnp.arange(slot_total, dtype=jnp.int32)[:, None]
    found = lax.optimization_barrier(
        jnp.sum(jnp.where(matches, entries[None, :], 0), axis=1, dtype=jnp.int32)
    )
    block_index = found % block_total
    slot_regrown = found // block_total & 1
    slot_last = found // block_total // 2
    live_count = jnp.sum(flags, dtype=jnp.int32)
    up_count = jnp.sum(flags[: block_total // 2], dtype=jnp.int32)
    return (block_index, slot_regrown, slot_last, live_count, up_count)


def adam_step(
    weights, first_in, second_in, block_grads, live_slots, slot_regrown, slot_last, step_value
):
    regrown_now = (slot_regrown == 1)[:, None, None]
    skipped = (step_value - slot_last - 1).astype(jnp.float32)[:, None, None]
    base_weight = jnp.where(regrown_now, jnp.float32(0.0), weights)
    kept_first = jnp.where(
        regrown_now, jnp.float32(0.0), first_in * jnp.power(jnp.float32(beta_one), skipped)
    )
    kept_second = jnp.where(
        regrown_now, jnp.float32(0.0), second_in * jnp.power(jnp.float32(beta_two), skipped)
    )
    new_first = beta_one * kept_first + (1.0 - beta_one) * block_grads
    new_second = beta_two * kept_second + (1.0 - beta_two) * block_grads * block_grads
    bias_count = jnp.where(
        regrown_now, jnp.float32(1.0), step_value.astype(jnp.float32) + jnp.zeros_like(skipped)
    )
    first_hat = new_first / (1.0 - jnp.power(jnp.float32(beta_one), bias_count))
    second_hat = new_second / (1.0 - jnp.power(jnp.float32(beta_two), bias_count))
    new_weight = base_weight - learn_rate * (
        first_hat / (jnp.sqrt(second_hat) + epsilon) + decay_rate * base_weight
    )
    keep_slot = live_slots[:, None, None]
    return (
        jnp.where(keep_slot, new_weight, weights),
        jnp.where(keep_slot, new_first, first_in),
        jnp.where(keep_slot, new_second, second_in),
    )


INNER = 2


def piece(index, chunk, chunks, shard):
    size = shard // chunks
    return pl.ds((index * chunks + chunk) * size, size)


def remote(src, dst, send_sem, recv_sem, axis, target):
    return pltpu.make_async_remote_copy(
        src_ref=src,
        dst_ref=dst,
        send_sem=send_sem,
        recv_sem=recv_sem,
        device_id={axis: target},
        device_id_type=pl.DeviceIdType.MESH,
    )


def greet(targets, meanwhile=None):
    barrier = pltpu.get_barrier_semaphore()
    for axis, target, exists in targets:

        @pl.when(exists)
        def _(axis=axis, target=target):
            pl.semaphore_signal(
                barrier, inc=1, device_id={axis: target}, device_id_type=pl.DeviceIdType.MESH
            )

    if meanwhile is not None:
        meanwhile()
    pl.semaphore_wait(barrier, sum(jnp.where(exists, 1, 0) for _, _, exists in targets))


class LineGather:
    def __init__(self, axis, size, chunks, own, out, sems):
        self.axis, self.chunks, self.own, self.out = axis, chunks, own, out
        self.recv, self.up, self.down, self.across, self.local = sems
        self.outer = size // INNER
        me = lax.axis_index(axis)
        self.me, self.mine, self.inner = me, me // INNER, me % INNER
        self.shard = own.shape[0]

    def targets(self):
        mine = self.mine
        return [
            (self.axis, self.me + INNER, mine + 1 < self.outer),
            (self.axis, self.me - INNER, mine > 0),
            (self.axis, mine * INNER + 1 - self.inner, mine >= 0),
        ]

    def copy(self, source, chunk, way, inner=None):
        inner = self.inner if inner is None else inner
        index = source * INNER + inner
        at = self.out.at[piece(index, chunk, self.chunks, self.shard)]
        slot = source * self.chunks + chunk
        sem, target = {
            "up": (self.up, self.me + INNER),
            "down": (self.down, self.me - INNER),
            "across": (self.across, self.mine * INNER + 1 - self.inner),
        }[way]
        recv = self.recv.at[index * self.chunks + chunk]
        return at, sem.at[slot], recv, target

    def send(self, source, chunk, way, own=False):
        at, sem, recv, target = self.copy(source, chunk, way)
        src = self.own.at[piece(0, chunk, self.chunks, self.shard)] if own else at
        remote(src, at, sem, recv, self.axis, target).start()

    def wait_send(self, source, chunk, way):
        at, sem, recv, target = self.copy(source, chunk, way)
        remote(at, at, sem, recv, self.axis, target).wait_send()

    def wait_recv(self, source, chunk, inner):
        at, sem, recv, target = self.copy(source, chunk, "across", inner)
        remote(at, at, sem, recv, self.axis, target).wait_recv()

    def own_copy(self):
        at = self.out.at[pl.ds(self.me * self.shard, self.shard)]
        return pltpu.make_async_copy(self.own, at, self.local)

    def begin(self, chunk):
        mine = self.mine

        @pl.when(mine + 1 < self.outer)
        def _():
            self.send(mine, chunk, "up", own=True)

        @pl.when(mine > 0)
        def _():
            self.send(mine, chunk, "down", own=True)

        self.send(mine, chunk, "across", own=True)

    def step(self, distance, chunk):
        low, high = self.mine - distance, self.mine + distance

        @pl.when(low >= 0)
        def _():
            self.wait_recv(low, chunk, self.inner)

            @pl.when(self.mine + 1 < self.outer)
            def _():
                self.send(low, chunk, "up")

            self.send(low, chunk, "across")

        @pl.when(high < self.outer)
        def _():
            self.wait_recv(high, chunk, self.inner)

            @pl.when(self.mine > 0)
            def _():
                self.send(high, chunk, "down")

            self.send(high, chunk, "across")

    def finish(self):
        for source in range(self.outer):
            for chunk in range(self.chunks):
                self.wait_recv(source, chunk, 1 - self.inner)
                self.wait_send(source, chunk, "across")

                @pl.when((self.mine >= source) & (self.mine + 1 < self.outer))
                def _(source=source, chunk=chunk):
                    self.wait_send(source, chunk, "up")

                @pl.when((self.mine <= source) & (self.mine > 0))
                def _(source=source, chunk=chunk):
                    self.wait_send(source, chunk, "down")

        self.own_copy().wait()


def gather_kernel(
    sizes,
    chunk_counts,
    weights,
    tokens,
    grad_out,
    packed_out,
    left_out,
    own_packed,
    own_left,
    *sems,
):
    lines = [
        LineGather("dp", sizes[0], chunk_counts[0], own_packed, packed_out, sems[:5]),
        LineGather("tensor", sizes[1], chunk_counts[1], own_left, left_out, sems[5:]),
    ]

    def round_own():
        side = own_left.shape[2]
        local_rows = own_left.shape[0] // 2
        for row in range(local_rows):
            own_left[row] = tokens[:, row * side : (row + 1) * side]
            own_left[local_rows + row] = grad_out[:, row * side : (row + 1) * side]

        def round_block(index, carry):
            own_packed[index] = weights[index].astype(jnp.bfloat16)
            return carry

        lax.fori_loop(0, own_packed.shape[0], round_block, 0)

    greet(lines[0].targets() + lines[1].targets(), round_own)
    events = []
    for line, weight in zip(lines, (1.5, 1.0)):
        for chunk in range(line.chunks):
            events.append((chunk / line.chunks, line, 0, chunk))
            for distance in range(1, line.outer):
                passed = (distance - 1 + (chunk + 1) / line.chunks) / (line.outer - 1)
                when = 1 + weight * passed
                events.append((when, line, distance, chunk))
    events.sort(key=lambda event: event[0])
    for when, line, distance, chunk in events:
        if distance == 0:
            line.begin(chunk)
    for line in lines:
        line.own_copy().start()
    for when, line, distance, chunk in events:
        if distance > 0:
            line.step(distance, chunk)
    for line in lines:
        line.finish()


def line_sems(size, chunks):
    dma = pltpu.SemaphoreType.DMA
    outer = size // INNER
    return [dma((size * chunks,))] + [dma((outer * chunks,))] * 3 + [dma]


def gather_all(weights, tokens, grad_out):
    sizes = (lax.axis_size("dp"), lax.axis_size("tensor"))
    side = weights.shape[1]
    own_left = (2 * tokens.shape[1] // side, tokens.shape[0], side)
    chunk_counts = (math.gcd(8, weights.shape[0]), math.gcd(4, own_left[0]))
    vmem = pl.BlockSpec(memory_space=pltpu.VMEM)
    anywhere = pl.BlockSpec(memory_space=pl.ANY)
    return pl.pallas_call(
        functools.partial(gather_kernel, sizes, chunk_counts),
        out_shape=(
            jax.ShapeDtypeStruct((sizes[0] * weights.shape[0], side, side), jnp.bfloat16),
            jax.ShapeDtypeStruct((sizes[1] * own_left[0],) + own_left[1:], jnp.bfloat16),
        ),
        in_specs=[vmem, vmem, vmem],
        out_specs=(anywhere, anywhere),
        scratch_shapes=[
            pltpu.VMEM(weights.shape, jnp.bfloat16),
            pltpu.VMEM(own_left, jnp.bfloat16),
        ]
        + line_sems(sizes[0], chunk_counts[0])
        + line_sems(sizes[1], chunk_counts[1]),
        compiler_params=pltpu.CompilerParams(
            collective_id=0, has_side_effects=True, vmem_limit_bytes=48 * 1024 * 1024
        ),
    )(weights, tokens, grad_out)


class PairReduce:
    def __init__(self, axis, size, chunks, data, out, near, far, sems):
        self.axis, self.chunks, self.data, self.out = axis, chunks, data, out
        self.near, self.far = near, far
        self.near_send, self.near_recv, self.far_send, self.far_recv = sems
        self.outer = size // INNER
        me = lax.axis_index(axis)
        self.me, self.mine, self.inner = me, me // INNER, me % INNER
        self.shard = out.shape[0]

    def owner(self, offset):
        return lax.rem(self.mine + offset, self.outer)

    def targets(self):
        far = [
            (self.axis, self.owner(offset) * INNER + self.inner, self.mine >= 0)
            for offset in range(1, self.outer)
        ]
        return far + [(self.axis, self.mine * INNER + 1 - self.inner, self.mine >= 0)]

    def near_copy(self, offset, chunk):
        owner = self.owner(offset)
        other = 1 - self.inner
        slot = owner * self.chunks + chunk
        return remote(
            self.data.at[piece(owner * INNER + other, chunk, self.chunks, self.shard)],
            self.near.at[piece(owner, chunk, self.chunks, self.shard)],
            self.near_send.at[slot],
            self.near_recv.at[slot],
            self.axis,
            self.mine * INNER + other,
        )

    def far_copy(self, offset, chunk):
        owner = self.owner(offset)
        return remote(
            self.near.at[piece(owner, chunk, self.chunks, self.shard)],
            self.far.at[piece(offset - 1, chunk, self.chunks, self.shard)],
            self.far_send.at[(offset - 1) * self.chunks + chunk],
            self.far_recv.at[(offset - 1) * self.chunks + chunk],
            self.axis,
            owner * INNER + self.inner,
        )

    def send_pair(self, offset, chunk):
        self.near_copy(offset, chunk).wait_recv()
        owner = self.owner(offset)
        size = self.shard // self.chunks
        near_at = (owner * self.chunks + chunk) * size
        data_at = ((owner * INNER + self.inner) * self.chunks + chunk) * size

        def add(index, carry):
            total = self.near[near_at + index].astype(jnp.float32)
            total += self.data[data_at + index].astype(jnp.float32)
            self.near[near_at + index] = total.astype(jnp.bfloat16)
            return carry

        lax.fori_loop(0, size, add, 0)
        self.far_copy(offset, chunk).start()

    def total(self, chunk):
        self.near_copy(0, chunk).wait_recv()
        for offset in range(1, self.outer):
            self.far_copy(offset, chunk).wait_recv()
        size = self.shard // self.chunks
        near_at = (self.mine * self.chunks + chunk) * size
        data_at = (self.me * self.chunks + chunk) * size

        def add(index, carry):
            total = self.near[near_at + index].astype(jnp.float32)
            total += self.data[data_at + index].astype(jnp.float32)
            for offset in range(1, self.outer):
                at = ((offset - 1) * self.chunks + chunk) * size
                total += self.far[at + index].astype(jnp.float32)
            self.out[chunk * size + index] = total.astype(self.out.dtype)
            return carry

        lax.fori_loop(0, size, add, 0)

    def finish(self):
        for chunk in range(self.chunks):
            for offset in range(self.outer):
                self.near_copy(offset, chunk).wait_send()
                if offset > 0:
                    self.far_copy(offset, chunk).wait_send()


def make_tiles(left_at, right_at, left_ref, right_ref, tiles_ref, first, count, scale):
    unroll = math.gcd(UNROLL, count)

    def step(index, carry):
        base = first + index * unroll
        for k in range(unroll):
            tile = lax.dot_general(
                left_ref[left_at[base + k]],
                right_ref[right_at[base + k]],
                (((0,), (0,)), ((), ())),
                preferred_element_type=jnp.float32,
            )
            tiles_ref[base + k] = (scale * tile).astype(jnp.bfloat16)
        return carry

    lax.fori_loop(0, count // unroll, step, 0)


def reduce_kernel(
    sizes,
    chunk_counts,
    scale,
    left_at,
    right_at,
    left_ref,
    right_ref,
    rows,
    grads_out,
    rows_out,
    tiles,
    *scratch,
):
    wide = PairReduce(
        "dp", sizes[0], chunk_counts[0], tiles, grads_out, scratch[0], scratch[1], scratch[4:8]
    )
    thin = PairReduce(
        "tensor", sizes[1], chunk_counts[1], rows, rows_out, scratch[2], scratch[3], scratch[8:]
    )
    greet(wide.targets() + thin.targets())
    for offset in list(range(1, thin.outer)) + [0]:
        for chunk in range(thin.chunks):
            thin.near_copy(offset, chunk).start()
    size = wide.shard // wide.chunks
    thin_pairs = [(o, k) for o in range(1, thin.outer) for k in range(thin.chunks)]
    wide_steps = [(o, k) for o in list(range(1, wide.outer)) + [0] for k in range(wide.chunks)]
    for at, (offset, chunk) in enumerate(wide_steps):
        owner = wide.owner(offset)
        for inner in (1 - wide.inner, wide.inner):
            first = ((owner * INNER + inner) * wide.chunks + chunk) * size
            make_tiles(left_at, right_at, left_ref, right_ref, tiles, first, size, scale)
            if inner is not wide.inner:
                wide.near_copy(offset, chunk).start()
        if offset > 0:
            wide.send_pair(offset, chunk)
        low = at * len(thin_pairs) // len(wide_steps)
        high = (at + 1) * len(thin_pairs) // len(wide_steps)
        for pair in thin_pairs[low:high]:
            thin.send_pair(*pair)
    for chunk in range(wide.chunks - 1):
        wide.total(chunk)
    for chunk in range(thin.chunks):
        thin.total(chunk)
    wide.total(wide.chunks - 1)
    wide.finish()
    thin.finish()


def pair_sems(size, chunks):
    dma = pltpu.SemaphoreType.DMA
    outer = size // INNER
    return [dma((outer * chunks,))] * 2 + [dma((max(outer - 1, 1) * chunks,))] * 2


def reduce_all(left_at, right_at, left_source, right_source, partial_rows, scale):
    sizes = (lax.axis_size("dp"), lax.axis_size("tensor"))
    side = left_source.shape[2]
    tile_shape = (left_at.shape[0], side, side)
    shards = (tile_shape[0] // sizes[0], partial_rows.shape[0] // sizes[1])
    chunk_counts = (math.gcd(8, shards[0]), math.gcd(2, shards[1]))
    vmem = pl.BlockSpec(memory_space=pltpu.VMEM)
    smem = pl.BlockSpec(memory_space=pltpu.SMEM)
    scratch = [pltpu.VMEM(tile_shape, jnp.bfloat16)]
    for shape, size, shard in zip((tile_shape, partial_rows.shape), sizes, shards):
        outer = size // INNER
        scratch.append(pltpu.VMEM((outer * shard,) + shape[1:], jnp.bfloat16))
        scratch.append(pltpu.VMEM((max(outer - 1, 1) * shard,) + shape[1:], jnp.bfloat16))
    return pl.pallas_call(
        functools.partial(reduce_kernel, sizes, chunk_counts, scale),
        out_shape=(
            jax.ShapeDtypeStruct((shards[0],) + tile_shape[1:], jnp.float32),
            jax.ShapeDtypeStruct((shards[1],) + partial_rows.shape[1:], jnp.bfloat16),
        ),
        in_specs=[smem, smem, vmem, vmem, vmem],
        out_specs=(vmem, vmem),
        scratch_shapes=scratch
        + pair_sems(sizes[0], chunk_counts[0])
        + pair_sems(sizes[1], chunk_counts[1]),
        compiler_params=pltpu.CompilerParams(
            collective_id=1, has_side_effects=True, vmem_limit_bytes=48 * 1024 * 1024
        ),
    )(left_at, right_at, left_source, right_source, partial_rows)


UNROLL = 8


def forward_kernel(
    left_at,
    right_at,
    sum_at,
    row_at,
    up_steps,
    packed_ref,
    left_ref,
    right_ref,
    out_ref,
    sums,
    row_sums,
    *,
    scale,
):
    slot_total = packed_ref.shape[0]
    columns = right_ref.shape[0] // 2

    def clear(index, carry):
        sums[index] = jnp.zeros(sums.shape[1:], jnp.float32)
        return carry

    lax.fori_loop(0, sums.shape[0], clear, 0)

    def add_slots(step, carry):
        base = step * UNROLL
        parts = [
            jnp.dot(
                left_ref[left_at[base + k]],
                packed_ref[base + k],
                preferred_element_type=jnp.float32,
            )
            for k in range(UNROLL)
        ]
        for k in range(UNROLL):
            sums[sum_at[base + k]] += parts[k]
        return carry

    lax.fori_loop(0, slot_total // UNROLL, add_slots, 0)

    def activate(column, carry):
        pre_act = scale * sums[column]
        back_act = scale * sums[columns + column]
        right_ref[column] = (back_act * silu_slope(pre_act)).astype(jnp.bfloat16)
        right_ref[columns + column] = jax.nn.silu(pre_act).astype(jnp.bfloat16)
        return carry

    lax.fori_loop(0, columns, activate, 0)

    add_input_grad(right_at, row_at, up_steps, packed_ref, right_ref, out_ref, row_sums, scale)


def add_input_grad(right_at, row_at, up_steps, packed_ref, right_ref, out_ref, sums, scale):
    rows = out_ref.shape[0]

    def clear(index, carry):
        sums[index] = jnp.zeros(sums.shape[1:], jnp.float32)
        return carry

    lax.fori_loop(0, rows, clear, 0)

    def add_slots(step, carry):
        base = step * UNROLL
        parts = [
            lax.dot_general(
                right_ref[right_at[base + k]],
                packed_ref[base + k],
                (((1,), (1,)), ((), ())),
                preferred_element_type=jnp.float32,
            )
            for k in range(UNROLL)
        ]
        for k in range(UNROLL):
            sums[row_at[base + k]] += parts[k]
        return carry

    lax.fori_loop(0, up_steps[0], add_slots, 0)

    def finish(index, carry):
        out_ref[index] = (scale * sums[index]).astype(jnp.bfloat16)
        return carry

    lax.fori_loop(0, rows, finish, 0)


def per_device(
    tokens,
    grad_out,
    packed_weight_blocks,
    packed_first_moments,
    packed_second_moments,
    block_mask,
    last_step,
    regrown,
    step_now,
):
    scale_factor = 3.0 / math.sqrt(D)
    tok_count = tokens.shape[0]
    owned_slots = packed_weight_blocks.shape[0]
    block_size = packed_weight_blocks.shape[1]
    row_blocks = block_mask.shape[1]
    column_blocks = block_mask.shape[2]
    local_rows = tokens.shape[1] // block_size
    groups = lax.axis_size("dp")
    slot_total = owned_slots * groups
    step_value = step_now[0]
    packed, left_source = gather_all(packed_weight_blocks, tokens, grad_out)
    block_index, slot_regrown, slot_last, live_count, up_count = slot_table(
        block_mask, regrown, last_step, slot_total
    )
    matrix_of = block_index // (row_blocks * column_blocks)
    row_of = block_index // column_blocks % row_blocks
    column_of = block_index % column_blocks
    slot_ids = jnp.arange(slot_total, dtype=jnp.int32)
    usable = (slot_ids < live_count) & (slot_regrown == 0)
    left_at = (row_of // local_rows * 2 + matrix_of) * local_rows + row_of % local_rows
    right_at = matrix_of * column_blocks + column_of
    sum_at = jnp.where(usable, right_at, 2 * column_blocks)
    row_at = jnp.where(usable & (matrix_of == 0), row_of, row_blocks)
    up_steps = ((up_count + UNROLL - 1) // UNROLL).reshape(1)
    smem = pl.BlockSpec(memory_space=pltpu.SMEM)
    vmem = pl.BlockSpec(memory_space=pltpu.VMEM)
    params = pltpu.CompilerParams(vmem_limit_bytes=48 * 1024 * 1024)
    block = (tok_count, block_size)
    right_source, partial_rows = pl.pallas_call(
        functools.partial(forward_kernel, scale=scale_factor),
        out_shape=(
            jax.ShapeDtypeStruct((2 * column_blocks,) + block, jnp.bfloat16),
            jax.ShapeDtypeStruct((row_blocks,) + block, jnp.bfloat16),
        ),
        in_specs=[smem] * 5 + [vmem] * 2,
        out_specs=(vmem, vmem),
        scratch_shapes=[
            pltpu.VMEM((2 * column_blocks + 1,) + block, jnp.float32),
            pltpu.VMEM((row_blocks + 1,) + block, jnp.float32),
        ],
        compiler_params=params,
    )(left_at, right_at, sum_at, row_at, up_steps, packed, left_source)
    block_grads, summed_rows = reduce_all(
        left_at, right_at, left_source, right_source, partial_rows, scale_factor
    )
    input_grad = (
        summed_rows.transpose(1, 0, 2).reshape(tok_count, tokens.shape[1]).astype(jnp.bfloat16)
    )
    owner_first = lax.axis_index("dp") * owned_slots
    mine_regrown = lax.dynamic_slice_in_dim(slot_regrown, owner_first, owned_slots)
    mine_last = lax.dynamic_slice_in_dim(slot_last, owner_first, owned_slots)
    live_slots = owner_first + jnp.arange(owned_slots, dtype=jnp.int32) < live_count
    new_weights, new_first, new_second = adam_step(
        packed_weight_blocks,
        packed_first_moments,
        packed_second_moments,
        block_grads,
        live_slots,
        mine_regrown,
        mine_last,
        step_value,
    )
    return (input_grad, new_weights, new_first, new_second)


def solution(mesh):
    in_specs = (
        P("dp", "tensor"),
        P("dp", "tensor"),
        P(("dp", "tensor"), None, None),
        P(("dp", "tensor"), None, None),
        P(("dp", "tensor"), None, None),
        P(None, None, "tensor"),
        P(None, None, "tensor"),
        P(None, None, "tensor"),
        P(),
    )
    out_specs = (
        P("dp", "tensor"),
        P(("dp", "tensor"), None, None),
        P(("dp", "tensor"), None, None),
        P(("dp", "tensor"), None, None),
    )
    return jax.shard_map(
        per_device, mesh=mesh, in_specs=in_specs, out_specs=out_specs, check_vma=False
    )
```

profile of v0, /device:TPU:0, one launch (start us, length us, event | category | flops | bytes accessed | tf_op | source)
XLA Modules:
  0.0 153.8 jit_solution(8211407244393025527)
XLA Ops:
  1.3 0.8 multiply_add_fusion.1
  2.0 0.1 copy.16
  2.1 0.1 reshape.52
  2.2 0.3 reduce-window.9
  2.5 0.1 slice.13
  2.6 0.1 slice_reduce_fusion
  2.7 0.6 broadcast_and_fusion
  3.4 0.7 add_compare_fusion
  4.0 0.6 slice_reduce_fusion.1
  5.3 0.3 select_reduce_fusion
  5.6 0.7 and_select_fusion.1
  6.3 0.7 broadcast_select_fusion
  7.0 0.1 power_subtract_fusion.1
  7.1 0.0 copy-start.1
  7.1 0.9 copy-done.1
  8.1 0.0 copy-start.2
  8.1 0.9 copy-done.2
  9.0 55.2 %shard_map.120 = (bf16[256,128,128]{2,1,0:T(8,128)(2,1)}, bf16[128,128,128]{2,1,0:T(8,128)(2,1)S(1)}) custom-call(f32[64,128,128]{2,1,0:T(8,128)} %weights.1, bf16[128,1024]{1,0:T(8,128)(2,1)S(1)} %copy-done.1, bf16[128,1024]{1,0:T(8,128)(2,1)S(1)} %copy-done.2), custom_call_target="tpu_custom_call" | custom-call | tf_op jit(solution)/shard_map/pallas_call | solution.py:274
  64.3 0.0 copy-start
  64.3 2.0 %copy-done = bf16[128,128,128]{2,1,0:T(8,128)(2,1)} copy-done((bf16[128,128,128]{2,1,0:T(8,128)(2,1)}, bf16[128,128,128]{2,1,0:T(8,128)(2,1)S(1)}, u32[]{:S(2)}) %copy-start) | copy-done | bytes 4194328
  66.3 18.3 %shard_map.121 = (bf16[32,128,128]{2,1,0:T(8,128)(2,1)S(1)}, bf16[64,128,128]{2,1,0:T(8,128)(2,1)S(1)}) custom-call(s32[256]{0:T(256)S(1)} %get-tuple-element.44.left_at, s32[256]{0:T(256)S(1)} %get-tuple-element.35.right_at, s32[256]{0:T(256)S(1)} %get-tuple-element.34.sum_at, s32[256]{0:T(256)S(1)} %get-tuple-element.30.row_at, s32[1]{0:T(128)} %bitcast.2.up_steps, ...), custom_call_target="tpu_custom_call" | custom-call | tf_op jit(solution)/shard_map/pallas_call | solution.py:611
  84.6 56.5 %shard_map.122 = (f32[64,128,128]{2,1,0:T(8,128)}, bf16[8,128,128]{2,1,0:T(8,128)(2,1)S(1)}) custom-call(s32[256]{0:T(256)S(1)} %get-tuple-element.44.left_at, s32[256]{0:T(256)S(1)} %get-tuple-element.35.right_at, bf16[128,128,128]{2,1,0:T(8,128)(2,1)} %copy-done, bf16[32,128,128]{2,1,0:T(8,128)(2,1)S(1)} %get-tuple-element.12.right_ref, ...), custom_call_target="tpu_custom_call" | custom-call | tf_op jit(solution)/shard_map/pallas_call | solution.py:467
  141.1 0.2 copy.17
  141.3 0.9 copy.18
  142.2 11.6 %fusion.2 = (f32[64,128,128]{2,1,0:T(8,128)}, f32[64,128,128]{2,1,0:T(8,128)}, f32[64,128,128]{2,1,0:T(8,128)}) fusion(f32[64,128,128]{2,1,0:T(8,128)} %param.13, f32[64,128,128]{2,1,0:T(8,128)} %get-tuple-element.15, f32[64]{0:T(128)S(1)} %convert_power_fusion, pred[64]{0:T(512)(128)(4,1)S(1)} %get-tuple-element.27, pred[64]{0:T(512)(128)(4,1)S(1)} %add_compare_fusion, ...), kind=kLoop, calls=%fused_computation.5 | loop fusion | flops 24117248 | bytes 29361280 | tf_op jit(solution)/shard_map/jit(_where)/select_n | solution.py:71
  (5 shorter events, 0.1 us)
Async XLA Ops:
  7.1 1.0 copy-start.1
  8.1 0.9 copy-start.2
  64.3 2.0 %copy-start = (bf16[128,128,128]{2,1,0:T(8,128)(2,1)}, bf16[128,128,128]{2,1,0:T(8,128)(2,1)S(1)}, u32[]{:S(2)}) copy-start(bf16[128,128,128]{2,1,0:T(8,128)(2,1)S(1)} %get-tuple-element.10.left_ref) | copy-start | bytes 12582916
where the time goes:
time: 154 us
  Pallas kernels  130 us (84%)
  other arithmetic  16.4 us (11%)
  local copies, waits for them, and re-layouts  5.29 us (3%)
  between operations  2.04 us (1%)
    pallas_call x1, Pallas kernels, reduce_all(): pl.pallas_call(functools.partial(reduce_kernel, sizes, chunk_counts, scal...  56.5 us
    pallas_call x1, Pallas kernels, gather_all(): pl.pallas_call(functools.partial(gather_kernel, sizes, chunk_counts), out...  55.2 us
    pallas_call x1, Pallas kernels, per_device(): pl.pallas_call(functools.partial(forward_kernel, scale=scale_factor), out...  18.3 us
    select_n x1, other arithmetic, adam_step(): jnp.where(keep_slot, new_second, second_in)  11.6 us
    unnamed x7, local copies, waits for them, and re-layouts  4.76 us

commit v1 on v0

v1 whole, which is shorter than its diff:
```python
import functools
import math

import jax
import jax.numpy as jnp
from jax import lax
from jax.experimental import pallas as pl
from jax.experimental.pallas import tpu as pltpu
from jax.sharding import PartitionSpec as P

D = 8192


beta_one = 0.9
beta_two = 0.95
learn_rate = 0.05
decay_rate = 0.1
epsilon = 0.05


def silu_slope(values):
    sigmoid = jax.nn.sigmoid(values)
    return sigmoid * (1.0 + values * (1.0 - sigmoid))


def slot_table(mask_grid, regrown_grid, last_grid, slot_total):
    codes = lax.optimization_barrier((mask_grid + 2 * regrown_grid + 4 * last_grid).reshape(-1))
    flags = codes & 1
    numbered = jnp.cumsum(flags, dtype=jnp.int32) - 1
    block_total = flags.shape[0]
    wanted = jnp.where(flags == 1, numbered, -1)
    entries = jnp.arange(block_total, dtype=jnp.int32) + block_total * (codes >> 1)
    matches = wanted[None, :] == jnp.arange(slot_total, dtype=jnp.int32)[:, None]
    found = lax.optimization_barrier(
        jnp.sum(jnp.where(matches, entries[None, :], 0), axis=1, dtype=jnp.int32)
    )
    block_index = found % block_total
    slot_regrown = found // block_total & 1
    slot_last = found // block_total // 2
    live_count = jnp.sum(flags, dtype=jnp.int32)
    up_count = jnp.sum(flags[: block_total // 2], dtype=jnp.int32)
    return (block_index, slot_regrown, slot_last, live_count, up_count)


def adam_step(
    weights, first_in, second_in, block_grads, live_slots, slot_regrown, slot_last, step_value
):
    regrown_now = (slot_regrown == 1)[:, None, None]
    skipped = (step_value - slot_last - 1).astype(jnp.float32)[:, None, None]
    base_weight = jnp.where(regrown_now, jnp.float32(0.0), weights)
    kept_first = jnp.where(
        regrown_now, jnp.float32(0.0), first_in * jnp.power(jnp.float32(beta_one), skipped)
    )
    kept_second = jnp.where(
        regrown_now, jnp.float32(0.0), second_in * jnp.power(jnp.float32(beta_two), skipped)
    )
    new_first = beta_one * kept_first + (1.0 - beta_one) * block_grads
    new_second = beta_two * kept_second + (1.0 - beta_two) * block_grads * block_grads
    bias_count = jnp.where(
        regrown_now, jnp.float32(1.0), step_value.astype(jnp.float32) + jnp.zeros_like(skipped)
    )
    first_hat = new_first / (1.0 - jnp.power(jnp.float32(beta_one), bias_count))
    second_hat = new_second / (1.0 - jnp.power(jnp.float32(beta_two), bias_count))
    new_weight = base_weight - learn_rate * (
        first_hat / (jnp.sqrt(second_hat) + epsilon) + decay_rate * base_weight
    )
    keep_slot = live_slots[:, None, None]
    return (
        jnp.where(keep_slot, new_weight, weights),
        jnp.where(keep_slot, new_first, first_in),
        jnp.where(keep_slot, new_second, second_in),
    )


INNER = 2
UNROLL = 8


def piece(index, chunk, chunks, shard):
    size = shard // chunks
    return pl.ds((index * chunks + chunk) * size, size)


def remote(src, dst, send_sem, recv_sem, axis, target):
    return pltpu.make_async_remote_copy(
        src_ref=src,
        dst_ref=dst,
        send_sem=send_sem,
        recv_sem=recv_sem,
        device_id={axis: target},
        device_id_type=pl.DeviceIdType.MESH,
    )


def greet(targets, meanwhile):
    barrier = pltpu.get_barrier_semaphore()
    for axis, target in targets:
        pl.semaphore_signal(
            barrier, inc=1, device_id={axis: target}, device_id_type=pl.DeviceIdType.MESH
        )
    meanwhile()
    pl.semaphore_wait(barrier, len(targets))


class LineGather:
    def __init__(self, axis, size, chunks, shard, out, sems):
        self.axis, self.chunks, self.out = axis, chunks, out
        self.recv, self.up, self.down, self.across = sems
        self.outer = size // INNER
        me = lax.axis_index(axis)
        self.me, self.mine, self.inner = me, me // INNER, me % INNER
        self.shard = shard

    def copy(self, source, chunk, way, inner=None):
        inner = self.inner if inner is None else inner
        index = source * INNER + inner
        at = self.out.at[piece(index, chunk, self.chunks, self.shard)]
        slot = source * self.chunks + chunk
        sem, target = {
            "up": (self.up, self.me + INNER),
            "down": (self.down, self.me - INNER),
            "across": (self.across, self.mine * INNER + 1 - self.inner),
        }[way]
        recv = self.recv.at[index * self.chunks + chunk]
        return remote(at, at, sem.at[slot], recv, self.axis, target)

    def wait_recv(self, source, chunk, inner):
        self.copy(source, chunk, "across", inner).wait_recv()

    def begin(self, chunk):
        mine = self.mine

        @pl.when(mine + 1 < self.outer)
        def _():
            self.copy(mine, chunk, "up").start()

        @pl.when(mine > 0)
        def _():
            self.copy(mine, chunk, "down").start()

        self.copy(mine, chunk, "across").start()

    def step(self, distance, chunk):
        low, high = self.mine - distance, self.mine + distance

        @pl.when(low >= 0)
        def _():
            self.wait_recv(low, chunk, self.inner)

            @pl.when(self.mine + 1 < self.outer)
            def _():
                self.copy(low, chunk, "up").start()

            self.copy(low, chunk, "across").start()

        @pl.when(high < self.outer)
        def _():
            self.wait_recv(high, chunk, self.inner)

            @pl.when(self.mine > 0)
            def _():
                self.copy(high, chunk, "down").start()

            self.copy(high, chunk, "across").start()

    def arrive(self, source):
        for chunk in range(self.chunks):
            self.wait_recv(source, chunk, 1 - self.inner)

    def finish(self):
        for source in range(self.outer):
            for chunk in range(self.chunks):
                self.copy(source, chunk, "across").wait_send()

                @pl.when((self.mine >= source) & (self.mine + 1 < self.outer))
                def _(source=source, chunk=chunk):
                    self.copy(source, chunk, "up").wait_send()

                @pl.when((self.mine <= source) & (self.mine > 0))
                def _(source=source, chunk=chunk):
                    self.copy(source, chunk, "down").wait_send()


class PairReduce:
    def __init__(self, axis, size, chunks, data, out, near, far, sems):
        self.axis, self.chunks, self.data, self.out = axis, chunks, data, out
        self.near, self.far = near, far
        self.near_send, self.near_recv, self.far_send, self.far_recv = sems
        self.outer = size // INNER
        me = lax.axis_index(axis)
        self.me, self.mine, self.inner = me, me // INNER, me % INNER
        self.shard = out.shape[0]
        self.size = self.shard // chunks

    def owner(self, offset):
        return lax.rem(self.mine + offset, self.outer)

    def targets(self):
        far = [
            (self.axis, self.owner(offset) * INNER + self.inner)
            for offset in range(1, self.outer)
        ]
        return far + [(self.axis, self.mine * INNER + 1 - self.inner)]

    def first(self, offset, chunk, inner):
        return ((self.owner(offset) * INNER + inner) * self.chunks + chunk) * self.size

    def near_copy(self, offset, chunk):
        owner = self.owner(offset)
        other = 1 - self.inner
        slot = owner * self.chunks + chunk
        return remote(
            self.data.at[piece(owner * INNER + other, chunk, self.chunks, self.shard)],
            self.near.at[piece(owner, chunk, self.chunks, self.shard)],
            self.near_send.at[slot],
            self.near_recv.at[slot],
            self.axis,
            self.mine * INNER + other,
        )

    def far_copy(self, offset, chunk):
        owner = self.owner(offset)
        return remote(
            self.near.at[piece(owner, chunk, self.chunks, self.shard)],
            self.far.at[piece(offset - 1, chunk, self.chunks, self.shard)],
            self.far_send.at[(offset - 1) * self.chunks + chunk],
            self.far_recv.at[(offset - 1) * self.chunks + chunk],
            self.axis,
            owner * INNER + self.inner,
        )

    def send_pair(self, offset, chunk):
        self.near_copy(offset, chunk).wait_recv()
        near_at = (self.owner(offset) * self.chunks + chunk) * self.size
        data_at = self.first(offset, chunk, self.inner)

        def add(index, carry):
            total = self.near[near_at + index].astype(jnp.float32)
            total += self.data[data_at + index].astype(jnp.float32)
            self.near[near_at + index] = total.astype(jnp.bfloat16)
            return carry

        lax.fori_loop(0, self.size, add, 0)
        self.far_copy(offset, chunk).start()

    def total(self, chunk):
        self.near_copy(0, chunk).wait_recv()
        for offset in range(1, self.outer):
            self.far_copy(offset, chunk).wait_recv()
        size = self.size
        near_at = (self.mine * self.chunks + chunk) * size
        data_at = (self.me * self.chunks + chunk) * size

        def add(index, carry):
            total = self.near[near_at + index].astype(jnp.float32)
            total += self.data[data_at + index].astype(jnp.float32)
            for offset in range(1, self.outer):
                at = ((offset - 1) * self.chunks + chunk) * size
                total += self.far[at + index].astype(jnp.float32)
            self.out[chunk * size + index] = total.astype(self.out.dtype)
            return carry

        lax.fori_loop(0, size, add, 0)

    def finish(self):
        for chunk in range(self.chunks):
            for offset in range(self.outer):
                self.near_copy(offset, chunk).wait_send()
                if offset > 0:
                    self.far_copy(offset, chunk).wait_send()


def chain_products(count, product, chain, table, previous):
    unroll = math.gcd(UNROLL, count)

    def step(index, carry):
        base = index * unroll
        parts = [product(base + k) for k in range(unroll)]
        for k in range(unroll):
            chain[base + k + 1] = parts[k] + chain[table[previous + base + k]]
        return carry

    lax.fori_loop(0, count // unroll, step, 0)


def make_tiles(table, right_table, left_ref, right_ref, tiles_ref, first, count, scale):
    unroll = math.gcd(UNROLL, count)

    def step(index, carry):
        base = first + index * unroll
        for k in range(unroll):
            tile = lax.dot_general(
                left_ref[table[base + k]],
                right_ref[table[right_table + base + k]],
                (((0,), (0,)), ((), ())),
                preferred_element_type=jnp.float32,
            )
            tiles_ref[base + k] = (scale * tile).astype(jnp.bfloat16)
        return carry

    lax.fori_loop(0, count // unroll, step, 0)


def step_kernel(
    sizes,
    gather_chunks,
    reduce_chunks,
    scale,
    table,
    weights,
    tokens,
    grad_out,
    grads_out,
    rows_out,
    packed,
    left,
    stage,
    chain,
    right,
    tiles,
    rows,
    wide_near,
    wide_far,
    thin_near,
    thin_far,
    *sems,
):
    local, sems = sems[:2], sems[2:]
    owned, side = stage.shape[0], stage.shape[1]
    slot_total, columns, row_blocks = packed.shape[0], right.shape[0] // 2, rows.shape[0]
    local_rows = rows_out.shape[0]
    line = LineGather("dp", sizes[0], gather_chunks[0], owned, packed, sems[:4])
    wing = LineGather("tensor", sizes[1], gather_chunks[1], 2 * local_rows, left, sems[4:8])
    wide = PairReduce(
        "dp", sizes[0], reduce_chunks[0], tiles, grads_out, wide_near, wide_far, sems[8:12]
    )
    thin = PairReduce(
        "tensor", sizes[1], reduce_chunks[1], rows, rows_out, thin_near, thin_far, sems[12:]
    )
    right_table = slot_total
    column_table = 2 * slot_total
    row_table = 3 * slot_total
    column_last = 4 * slot_total
    row_last = column_last + 2 * columns

    def load_left(index):
        source = tokens if index < local_rows else grad_out
        return pltpu.make_async_copy(
            source.at[:, pl.ds(index % local_rows * side, side)],
            left.at[wing.me * 2 * local_rows + index],
            local[0].at[index],
        )

    def load_weights(chunk):
        at = piece(0, chunk, line.chunks, owned)
        return pltpu.make_async_copy(weights.at[at], stage.at[at], local[1].at[chunk])

    def round_weights(chunk):
        load_weights(chunk).wait()
        size = owned // line.chunks
        at = chunk * size
        mine = line.me * owned + at

        def round_block(index, carry):
            packed[mine + index] = stage[at + index].astype(jnp.bfloat16)
            return carry

        lax.fori_loop(0, size, round_block, 0)

    for index in range(2 * local_rows):
        load_left(index).start()
    for chunk in range(line.chunks):
        load_weights(chunk).start()

    def meanwhile():
        chain[0] = jnp.zeros(chain.shape[1:], jnp.float32)
        for index in range(2 * local_rows):
            load_left(index).wait()
        for chunk in range(line.chunks):
            round_weights(chunk)

    greet(wide.targets() + thin.targets(), meanwhile)

    events = []
    for gather, weight in ((line, 1.5), (wing, 1.0)):
        for chunk in range(gather.chunks):
            gather.begin(chunk)
            for distance in range(1, gather.outer):
                passed = (distance - 1 + (chunk + 1) / gather.chunks) / (gather.outer - 1)
                events.append((weight * passed, gather, distance, chunk))
    events.sort(key=lambda event: event[0])
    for _, gather, distance, chunk in events:
        gather.step(distance, chunk)
    for source in range(wing.outer):
        wing.arrive(source)
    for source in range(line.outer):
        line.arrive(source)

    def forward(slot):
        return jnp.dot(
            left[table[slot]], packed[slot], preferred_element_type=jnp.float32
        )

    chain_products(slot_total, forward, chain, table, column_table)

    def activate(column, carry):
        pre_act = scale * chain[table[column_last + column]]
        back_act = scale * chain[table[column_last + columns + column]]
        right[column] = (back_act * silu_slope(pre_act)).astype(jnp.bfloat16)
        right[columns + column] = jax.nn.silu(pre_act).astype(jnp.bfloat16)
        return carry

    lax.fori_loop(0, columns, activate, 0)

    def backward(slot):
        return lax.dot_general(
            right[table[right_table + slot]],
            packed[slot],
            (((1,), (1,)), ((), ())),
            preferred_element_type=jnp.float32,
        )

    def sum_rows():
        chain_products(slot_total, backward, chain, table, row_table)

        def finish(index, carry):
            rows[index] = (scale * chain[table[row_last + index]]).astype(jnp.bfloat16)
            return carry

        lax.fori_loop(0, row_blocks, finish, 0)
        for offset in list(range(1, thin.outer)) + [0]:
            for chunk in range(thin.chunks):
                thin.near_copy(offset, chunk).start()

    def tiles_of(offset, chunk, inner):
        first = wide.first(offset, chunk, inner)
        make_tiles(table, right_table, left, right, tiles, first, wide.size, scale)

    far_steps = [(o, k) for o in range(1, wide.outer) for k in range(wide.chunks)]
    last_far = len(far_steps) - 1
    for at, step in enumerate(far_steps):
        tiles_of(*step, 1 - wide.inner)
        wide.near_copy(*step).start()
        if at > 0:
            wide.send_pair(*far_steps[at - 1])
        tiles_of(*step, wide.inner)
        if at == min(2, last_far):
            sum_rows()
    wide.send_pair(*far_steps[-1])
    thin_pairs = [(o, k) for o in range(1, thin.outer) for k in range(thin.chunks)]
    for chunk in range(wide.chunks):
        tiles_of(0, chunk, 1 - wide.inner)
        wide.near_copy(0, chunk).start()
        tiles_of(0, chunk, wide.inner)
        low = chunk * len(thin_pairs) // wide.chunks
        high = (chunk + 1) * len(thin_pairs) // wide.chunks
        for pair in thin_pairs[low:high]:
            thin.send_pair(*pair)
    for chunk in range(wide.chunks - 1):
        wide.total(chunk)
    for chunk in range(thin.chunks):
        thin.total(chunk)
    wide.total(wide.chunks - 1)
    line.finish()
    wing.finish()
    wide.finish()
    thin.finish()


def run_step(table, weights, tokens, grad_out, columns, row_blocks, scale):
    sizes = (lax.axis_size("dp"), lax.axis_size("tensor"))
    owned, side = weights.shape[0], weights.shape[1]
    tok_count = tokens.shape[0]
    local_rows = tokens.shape[1] // side
    slot_total = owned * sizes[0]
    outer = [size // INNER for size in sizes]
    gather_chunks = (math.gcd(8, owned), math.gcd(4, 2 * local_rows))
    reduce_chunks = (math.gcd(8, owned), math.gcd(2, local_rows))
    block = (tok_count, side)
    tile = (side, side)
    dma = pltpu.SemaphoreType.DMA

    def scratch(count, shape, kind=jnp.bfloat16):
        return pltpu.VMEM((count,) + shape, kind)

    shapes = [
        scratch(slot_total, tile),
        scratch(2 * local_rows * sizes[1], block),
        scratch(owned, tile, jnp.float32),
        scratch(slot_total + 1, block, jnp.float32),
        scratch(2 * columns, block),
        scratch(slot_total, tile),
        scratch(row_blocks, block),
        scratch(outer[0] * owned, tile),
        scratch(max(outer[0] - 1, 1) * owned, tile),
        scratch(outer[1] * local_rows, block),
        scratch(max(outer[1] - 1, 1) * local_rows, block),
        dma((2 * local_rows,)),
        dma((gather_chunks[0],)),
    ]
    for size, chunks in zip(sizes, gather_chunks):
        shapes += [dma((size * chunks,))] + [dma((size // INNER * chunks,))] * 3
    for count, chunks in zip(outer, reduce_chunks):
        shapes += [dma((count * chunks,))] * 2 + [dma((max(count - 1, 1) * chunks,))] * 2
    vmem = pl.BlockSpec(memory_space=pltpu.VMEM)
    smem = pl.BlockSpec(memory_space=pltpu.SMEM)
    anywhere = pl.BlockSpec(memory_space=pl.ANY)
    return pl.pallas_call(
        functools.partial(step_kernel, sizes, gather_chunks, reduce_chunks, scale),
        out_shape=(
            jax.ShapeDtypeStruct((owned,) + tile, jnp.float32),
            jax.ShapeDtypeStruct((local_rows,) + block, jnp.bfloat16),
        ),
        in_specs=[smem, anywhere, anywhere, anywhere],
        out_specs=(vmem, vmem),
        scratch_shapes=shapes,
        compiler_params=pltpu.CompilerParams(
            collective_id=0, has_side_effects=True, vmem_limit_bytes=62 * 1024 * 1024
        ),
    )(table, weights, tokens, grad_out)


def last_where(matches):
    places = jnp.arange(1, matches.shape[1] + 1, dtype=jnp.int32)
    return jnp.max(jnp.where(matches, places[None, :], 0), axis=1)


def per_device(
    tokens,
    grad_out,
    packed_weight_blocks,
    packed_first_moments,
    packed_second_moments,
    block_mask,
    last_step,
    regrown,
    step_now,
):
    scale_factor = 3.0 / math.sqrt(D)
    tok_count = tokens.shape[0]
    owned_slots = packed_weight_blocks.shape[0]
    block_size = packed_weight_blocks.shape[1]
    row_blocks = block_mask.shape[1]
    column_blocks = block_mask.shape[2]
    local_rows = tokens.shape[1] // block_size
    groups = lax.axis_size("dp")
    slot_total = owned_slots * groups
    step_value = step_now[0]
    block_index, slot_regrown, slot_last, live_count, _ = slot_table(
        block_mask, regrown, last_step, slot_total
    )
    matrix_of = block_index // (row_blocks * column_blocks)
    row_of = block_index // column_blocks % row_blocks
    column_of = block_index % column_blocks
    slot_ids = jnp.arange(slot_total, dtype=jnp.int32)
    usable = (slot_ids < live_count) & (slot_regrown == 0)
    left_at = (row_of // local_rows * 2 + matrix_of) * local_rows + row_of % local_rows
    right_at = matrix_of * column_blocks + column_of
    column_key = jnp.where(usable, right_at, -1)
    row_key = jnp.where(usable & (matrix_of == 0), row_of, -1)
    earlier = slot_ids[None, :] < slot_ids[:, None]
    table = jnp.concatenate(
        [
            left_at,
            right_at,
            last_where((right_at[:, None] == column_key[None, :]) & earlier),
            last_where((row_of[:, None] == row_key[None, :]) & earlier),
            last_where(jnp.arange(2 * column_blocks, dtype=jnp.int32)[:, None] == column_key),
            last_where(jnp.arange(row_blocks, dtype=jnp.int32)[:, None] == row_key),
        ]
    )
    block_grads, summed_rows = run_step(
        table,
        packed_weight_blocks,
        tokens,
        grad_out,
        column_blocks,
        row_blocks,
        scale_factor,
    )
    input_grad = (
        summed_rows.transpose(1, 0, 2).reshape(tok_count, tokens.shape[1]).astype(jnp.bfloat16)
    )
    owner_first = lax.axis_index("dp") * owned_slots
    mine_regrown = lax.dynamic_slice_in_dim(slot_regrown, owner_first, owned_slots)
    mine_last = lax.dynamic_slice_in_dim(slot_last, owner_first, owned_slots)
    live_slots = owner_first + jnp.arange(owned_slots, dtype=jnp.int32) < live_count
    new_weights, new_first, new_second = adam_step(
        packed_weight_blocks,
        packed_first_moments,
        packed_second_moments,
        block_grads,
        live_slots,
        mine_regrown,
        mine_last,
        step_value,
    )
    return (input_grad, new_weights, new_first, new_second)


def solution(mesh):
    in_specs = (
        P("dp", "tensor"),
        P("dp", "tensor"),
        P(("dp", "tensor"), None, None),
        P(("dp", "tensor"), None, None),
        P(("dp", "tensor"), None, None),
        P(None, None, "tensor"),
        P(None, None, "tensor"),
        P(None, None, "tensor"),
        P(),
    )
    out_specs = (
        P("dp", "tensor"),
        P(("dp", "tensor"), None, None),
        P(("dp", "tensor"), None, None),
        P(("dp", "tensor"), None, None),
    )
    return jax.shard_map(
        per_device, mesh=mesh, in_specs=in_specs, out_specs=out_specs, check_vma=False
    )
```

time: 154 us -> 136 us (0.88)
  Pallas kernels: 130 us -> 115 us
  local copies, waits for them, and re-layouts: 5.29 us -> 3.01 us
    pallas_call x3 -> x1, Pallas kernels: 130 us -> 115 us  [run_step(): pl.pallas_call(functools.partial(step_kernel, sizes, gather_chunks, reduc...]
    unnamed x7 -> x1, local copies, waits for them, and re-layouts: 4.76 us -> 0.85 us
where the time goes in v1:
time: 136 us
  Pallas kernels  115 us (85%)
  other arithmetic  16.3 us (12%)
  local copies, waits for them, and re-layouts  3.01 us (2%)
    pallas_call x1, Pallas kernels, run_step(): pl.pallas_call(functools.partial(step_kernel, sizes, gather_chunks, reduc...  115 us
    select_n x1, other arithmetic, adam_step(): jnp.where(keep_slot, new_second, second_in)  11.6 us

profile of v1, /device:TPU:0, one launch (start us, length us, event | category | flops | bytes accessed | tf_op | source)
XLA Modules:
  0.0 135.9 jit_solution(2612515276412865180)
XLA Ops:
  1.3 0.8 multiply_add_fusion.1
  2.0 0.1 copy.16
  2.1 0.1 reshape.57
  2.2 0.6 and_reduce_fusion
  2.9 0.7 add_compare_fusion
  3.5 0.3 reduce-window.9
  3.8 0.1 slice.9
  3.9 0.1 slice_reduce_fusion
  4.0 0.1 bitcast_select_fusion
  4.1 0.3 select_reduce_fusion
  4.4 0.7 broadcast_select_fusion
  5.1 0.1 power_subtract_fusion.1
  5.2 0.7 and_select_fusion.1
  5.9 0.1 select_reduce_fusion.3
  6.0 0.3 select_reduce_fusion.1
  6.3 0.1 select_reduce_fusion.4
  6.4 0.7 concatenate.3.table
  7.1 115.2 %shard_map.120 = (f32[64,128,128]{2,1,0:T(8,128)}, bf16[8,128,128]{2,1,0:T(8,128)(2,1)}) custom-call(s32[1120]{0:T(1024)} %concatenate.3.table, f32[64,128,128]{2,1,0:T(8,128)} %weights.1, bf16[128,1024]{1,0:T(8,128)(2,1)} %tokens.1, bf16[128,1024]{1,0:T(8,128)(2,1)} %grad_out.1), custom_call_target="tpu_custom_call" | custom-call | tf_op jit(solution)/shard_map/pallas_call | solution.py:508
  122.3 1.1 copy.17
  123.4 0.9 copy.18
  124.3 11.6 %fusion.2 = (f32[64,128,128]{2,1,0:T(8,128)}, f32[64,128,128]{2,1,0:T(8,128)}, f32[64,128,128]{2,1,0:T(8,128)}) fusion(f32[64,128,128]{2,1,0:T(8,128)} %param.13, f32[64,128,128]{2,1,0:T(8,128)} %get-tuple-element.7, f32[64]{0:T(128)S(1)} %convert_power_fusion, pred[64]{0:T(512)(128)(4,1)S(1)} %get-tuple-element.21, pred[64]{0:T(512)(128)(4,1)S(1)} %add_compare_fusion, ...), kind=kLoop, calls=%fused_computation.5 | loop fusion | flops 24117248 | bytes 29361280 | tf_op jit(solution)/shard_map/jit(_where)/select_n | solution.py:71
  (5 shorter events, 0.1 us)

commit v2 on v1

--- a/solution.py
+++ b/solution.py
@@ -23,53 +23,84 @@
     return sigmoid * (1.0 + values * (1.0 - sigmoid))
 
 
-def slot_table(mask_grid, regrown_grid, last_grid, slot_total):
-    codes = lax.optimization_barrier((mask_grid + 2 * regrown_grid + 4 * last_grid).reshape(-1))
-    flags = codes & 1
-    numbered = jnp.cumsum(flags, dtype=jnp.int32) - 1
-    block_total = flags.shape[0]
-    wanted = jnp.where(flags == 1, numbered, -1)
-    entries = jnp.arange(block_total, dtype=jnp.int32) + block_total * (codes >> 1)
-    matches = wanted[None, :] == jnp.arange(slot_total, dtype=jnp.int32)[:, None]
-    found = lax.optimization_barrier(
-        jnp.sum(jnp.where(matches, entries[None, :], 0), axis=1, dtype=jnp.int32)
-    )
-    block_index = found % block_total
-    slot_regrown = found // block_total & 1
-    slot_last = found // block_total // 2
-    live_count = jnp.sum(flags, dtype=jnp.int32)
-    up_count = jnp.sum(flags[: block_total // 2], dtype=jnp.int32)
-    return (block_index, slot_regrown, slot_last, live_count, up_count)
-
-
-def adam_step(
-    weights, first_in, second_in, block_grads, live_slots, slot_regrown, slot_last, step_value
-):
-    regrown_now = (slot_regrown == 1)[:, None, None]
-    skipped = (step_value - slot_last - 1).astype(jnp.float32)[:, None, None]
-    base_weight = jnp.where(regrown_now, jnp.float32(0.0), weights)
-    kept_first = jnp.where(
-        regrown_now, jnp.float32(0.0), first_in * jnp.power(jnp.float32(beta_one), skipped)
-    )
-    kept_second = jnp.where(
-        regrown_now, jnp.float32(0.0), second_in * jnp.power(jnp.float32(beta_two), skipped)
-    )
-    new_first = beta_one * kept_first + (1.0 - beta_one) * block_grads
-    new_second = beta_two * kept_second + (1.0 - beta_two) * block_grads * block_grads
-    bias_count = jnp.where(
-        regrown_now, jnp.float32(1.0), step_value.astype(jnp.float32) + jnp.zeros_like(skipped)
-    )
-    first_hat = new_first / (1.0 - jnp.power(jnp.float32(beta_one), bias_count))
-    second_hat = new_second / (1.0 - jnp.power(jnp.float32(beta_two), bias_count))
-    new_weight = base_weight - learn_rate * (
-        first_hat / (jnp.sqrt(second_hat) + epsilon) + decay_rate * base_weight
-    )
-    keep_slot = live_slots[:, None, None]
-    return (
-        jnp.where(keep_slot, new_weight, weights),
-        jnp.where(keep_slot, new_first, first_in),
-        jnp.where(keep_slot, new_second, second_in),
-    )
+def last_place(matches, places):
+    return jnp.max(jnp.where(matches, places, 0), axis=0, keepdims=True)
+
+
+def build_tables(mask, regrown, last_step, step_now, places, factors, sources, local_rows):
+    columns, rows = mask.shape[1:]
+    width = places.shape[1]
+    right_bits = (2 * columns - 1).bit_length()
+    left_bits = (2 * rows - 1).bit_length()
+
+    def row_source(row):
+        source = jnp.zeros_like(row)
+        for at in range(1, sources):
+            source += jnp.where(row >= at * local_rows, 1, 0)
+        return source
+
+    row = lax.broadcasted_iota(jnp.int32, (1, rows), 1)
+    source = row_source(row)
+    before = lax.broadcasted_iota(jnp.int32, (rows, rows), 0)
+    after = lax.broadcasted_iota(jnp.int32, (rows, rows), 1)
+    slots = lax.broadcasted_iota(jnp.int32, (width, rows), 0)
+    codes = jnp.zeros((width, rows), jnp.int32)
+    base = jnp.zeros((1, 1), jnp.int32)
+    for matrix in range(2):
+        counts = jnp.sum(mask[matrix], axis=0, keepdims=True)
+        spread = jnp.broadcast_to(counts, (rows, rows)).T
+        running = base + jnp.sum(jnp.where(before < after, spread, 0), axis=0, keepdims=True)
+        left_code = (row + (source + matrix) * local_rows) << right_bits
+        for column in range(columns):
+            flag = mask[matrix, column : column + 1, :]
+            state = (
+                1
+                + 2 * regrown[matrix, column : column + 1, :]
+                + 4 * last_step[matrix, column : column + 1, :]
+            )
+            code = matrix * columns + column + left_code + (state << (right_bits + left_bits))
+            wanted = jnp.where(flag == 1, running, -1)
+            codes += jnp.where(slots == wanted, code, 0)
+            running += flag
+        base += jnp.sum(counts, axis=1, keepdims=True)
+
+    def fields(code):
+        state = code >> (right_bits + left_bits)
+        right = code & ((1 << right_bits) - 1)
+        left = (code >> right_bits) & ((1 << left_bits) - 1)
+        return right, left, state & 1, (state >> 1) & 1, state >> 2
+
+    right, left, live, fresh, last = fields(jnp.sum(codes.T, axis=0, keepdims=True))
+    right_down, left_down, live_down, fresh_down, _ = fields(
+        jnp.sum(codes, axis=1, keepdims=True)
+    )
+    usable = (live_down == 1) & (fresh_down == 0)
+    column_key = jnp.where(usable, right_down, -1)
+    row_key = jnp.where(usable & (right_down < columns), left_down, -1)
+    down = lax.broadcasted_iota(jnp.int32, (width, width), 0)
+    across = lax.broadcasted_iota(jnp.int32, (width, width), 1)
+    place = down + 1
+    earlier = down < across
+    lane = lax.broadcasted_iota(jnp.int32, (1, width), 1)
+    lane_left = lane + row_source(lane) * local_rows
+    places[0:1, :] = left
+    places[1:2, :] = right
+    places[2:3, :] = last_place((column_key == right) & earlier, place)
+    places[3:4, :] = last_place((row_key == left) & earlier, place)
+    places[4:5, :] = last_place(column_key == lane, place)
+    places[5:6, :] = last_place(row_key == lane_left, place)
+    places[6:7, :] = live
+    places[7:8, :] = fresh
+    step = step_now[0]
+    skipped = (step - last - 1).astype(jnp.float32)
+    count = jnp.where(fresh == 1, 1, step).astype(jnp.float32)
+    for at, beta in ((0, beta_one), (2, beta_two)):
+        kept = beta * jnp.exp(skipped * math.log(beta))
+        factors[at : at + 1, :] = jnp.where(fresh == 1, 0.0, kept)
+        factors[at + 1 : at + 2, :] = 1.0 / (1.0 - jnp.exp(count * math.log(beta)))
+
+
+LEFT, RIGHT, COLUMN_BEFORE, ROW_BEFORE, COLUMN_LAST, ROW_LAST, LIVE, FRESH = range(8)
 
 
 INNER = 2
@@ -182,15 +213,15 @@
 
 
 class PairReduce:
-    def __init__(self, axis, size, chunks, data, out, near, far, sems):
-        self.axis, self.chunks, self.data, self.out = axis, chunks, data, out
+    def __init__(self, axis, size, chunks, data, shard, near, far, sems):
+        self.axis, self.chunks, self.data = axis, chunks, data
         self.near, self.far = near, far
         self.near_send, self.near_recv, self.far_send, self.far_recv = sems
         self.outer = size // INNER
         me = lax.axis_index(axis)
         self.me, self.mine, self.inner = me, me // INNER, me % INNER
-        self.shard = out.shape[0]
-        self.size = self.shard // chunks
+        self.shard = shard
+        self.size = shard // chunks
 
     def owner(self, offset):
         return lax.rem(self.mine + offset, self.outer)
@@ -243,7 +274,7 @@
         lax.fori_loop(0, self.size, add, 0)
         self.far_copy(offset, chunk).start()
 
-    def total(self, chunk):
+    def total(self, chunk, store):
         self.near_copy(0, chunk).wait_recv()
         for offset in range(1, self.outer):
             self.far_copy(offset, chunk).wait_recv()
@@ -257,7 +288,7 @@
             for offset in range(1, self.outer):
                 at = ((offset - 1) * self.chunks + chunk) * size
                 total += self.far[at + index].astype(jnp.float32)
-            self.out[chunk * size + index] = total.astype(self.out.dtype)
+            store(chunk * size + index, total)
             return carry
 
         lax.fori_loop(0, size, add, 0)
@@ -277,21 +308,21 @@
         base = index * unroll
         parts = [product(base + k) for k in range(unroll)]
         for k in range(unroll):
-            chain[base + k + 1] = parts[k] + chain[table[previous + base + k]]
+            chain[base + k + 1] = parts[k] + chain[table[previous, base + k]]
         return carry
 
     lax.fori_loop(0, count // unroll, step, 0)
 
 
-def make_tiles(table, right_table, left_ref, right_ref, tiles_ref, first, count, scale):
+def make_tiles(table, left_ref, right_ref, tiles_ref, first, count, scale):
     unroll = math.gcd(UNROLL, count)
 
     def step(index, carry):
         base = first + index * unroll
         for k in range(unroll):
             tile = lax.dot_general(
-                left_ref[table[base + k]],
-                right_ref[table[right_table + base + k]],
+                left_ref[table[LEFT, base + k]],
+                right_ref[table[RIGHT, base + k]],
                 (((0,), (0,)), ((), ())),
                 preferred_element_type=jnp.float32,
             )
@@ -306,15 +337,21 @@
     gather_chunks,
     reduce_chunks,
     scale,
-    table,
     weights,
+    first_in,
+    second_in,
     tokens,
     grad_out,
-    grads_out,
+    mask,
+    regrown,
+    last_step,
+    step_now,
     rows_out,
+    new_weights,
+    new_first,
+    new_second,
     packed,
     left,
-    stage,
     chain,
     right,
     tiles,
@@ -323,25 +360,24 @@
     wide_far,
     thin_near,
     thin_far,
+    places,
+    factors,
+    table,
+    factor,
     *sems,
 ):
-    local, sems = sems[:2], sems[2:]
-    owned, side = stage.shape[0], stage.shape[1]
+    local, sems = sems[:3], sems[3:]
+    owned, side = new_weights.shape[0], new_weights.shape[1]
     slot_total, columns, row_blocks = packed.shape[0], right.shape[0] // 2, rows.shape[0]
-    local_rows = rows_out.shape[0]
+    local_rows = rows_out.shape[1] // side
     line = LineGather("dp", sizes[0], gather_chunks[0], owned, packed, sems[:4])
     wing = LineGather("tensor", sizes[1], gather_chunks[1], 2 * local_rows, left, sems[4:8])
     wide = PairReduce(
-        "dp", sizes[0], reduce_chunks[0], tiles, grads_out, wide_near, wide_far, sems[8:12]
+        "dp", sizes[0], reduce_chunks[0], tiles, owned, wide_near, wide_far, sems[8:12]
     )
     thin = PairReduce(
-        "tensor", sizes[1], reduce_chunks[1], rows, rows_out, thin_near, thin_far, sems[12:]
-    )
-    right_table = slot_total
-    column_table = 2 * slot_total
-    row_table = 3 * slot_total
-    column_last = 4 * slot_total
-    row_last = column_last + 2 * columns
+        "tensor", sizes[1], reduce_chunks[1], rows, local_rows, thin_near, thin_far, sems[12:]
+    )
 
     def load_left(index):
         source = tokens if index < local_rows else grad_out
@@ -353,7 +389,7 @@
 
     def load_weights(chunk):
         at = piece(0, chunk, line.chunks, owned)
-        return pltpu.make_async_copy(weights.at[at], stage.at[at], local[1].at[chunk])
+        return pltpu.make_async_copy(weights.at[at], new_weights.at[at], local[1].at[chunk])
 
     def round_weights(chunk):
         load_weights(chunk).wait()
@@ -362,35 +398,57 @@
         mine = line.me * owned + at
 
         def round_block(index, carry):
-            packed[mine + index] = stage[at + index].astype(jnp.bfloat16)
+            packed[mine + index] = new_weights[at + index].astype(jnp.bfloat16)
             return carry
 
         lax.fori_loop(0, size, round_block, 0)
 
-    for index in range(2 * local_rows):
-        load_left(index).start()
-    for chunk in range(line.chunks):
-        load_weights(chunk).start()
+    moments = [
+        pltpu.make_async_copy(first_in, new_first, local[2].at[0]),
+        pltpu.make_async_copy(second_in, new_second, local[2].at[1]),
+    ]
+    load_tables = [
+        pltpu.make_async_copy(places, table, local[2].at[2]),
+        pltpu.make_async_copy(factors, factor, local[2].at[3]),
+    ]
 
     def meanwhile():
-        chain[0] = jnp.zeros(chain.shape[1:], jnp.float32)
+        load_weights(0).start()
+        for index in range(2 * local_rows):
+            load_left(index).start()
+        for chunk in range(1, line.chunks):
+            load_weights(chunk).start()
+        round_weights(0)
         for index in range(2 * local_rows):
             load_left(index).wait()
-        for chunk in range(line.chunks):
-            round_weights(chunk)
 
     greet(wide.targets() + thin.targets(), meanwhile)
+    line.begin(0)
+    for chunk in range(wing.chunks):
+        wing.begin(chunk)
+    for chunk in range(1, line.chunks):
+        round_weights(chunk)
+        line.begin(chunk)
+    for copy in moments:
+        copy.start()
+    chain[0] = jnp.zeros(chain.shape[1:], jnp.float32)
+    build_tables(
+        mask, regrown, last_step, step_now, places, factors, sizes[1], local_rows
+    )
+    for copy in load_tables:
+        copy.start()
 
     events = []
     for gather, weight in ((line, 1.5), (wing, 1.0)):
         for chunk in range(gather.chunks):
-            gather.begin(chunk)
             for distance in range(1, gather.outer):
                 passed = (distance - 1 + (chunk + 1) / gather.chunks) / (gather.outer - 1)
                 events.append((weight * passed, gather, distance, chunk))
     events.sort(key=lambda event: event[0])
     for _, gather, distance, chunk in events:
         gather.step(distance, chunk)
+    for copy in load_tables:
+        copy.wait()
     for source in range(wing.outer):
         wing.arrive(source)
     for source in range(line.outer):
@@ -398,14 +456,14 @@
 
     def forward(slot):
         return jnp.dot(
-            left[table[slot]], packed[slot], preferred_element_type=jnp.float32
+            left[table[LEFT, slot]], packed[slot], preferred_element_type=jnp.float32
         )
 
-    chain_products(slot_total, forward, chain, table, column_table)
+    chain_products(slot_total, forward, chain, table, COLUMN_BEFORE)
 
     def activate(column, carry):
-        pre_act = scale * chain[table[column_last + column]]
-        back_act = scale * chain[table[column_last + columns + column]]
+        pre_act = scale * chain[table[COLUMN_LAST, column]]
+        back_act = scale * chain[table[COLUMN_LAST, columns + column]]
         right[column] = (back_act * silu_slope(pre_act)).astype(jnp.bfloat16)
         right[columns + column] = jax.nn.silu(pre_act).astype(jnp.bfloat16)
         return carry
@@ -414,17 +472,17 @@
 
     def backward(slot):
         return lax.dot_general(
-            right[table[right_table + slot]],
+            right[table[RIGHT, slot]],
             packed[slot],
             (((1,), (1,)), ((), ())),
             preferred_element_type=jnp.float32,
         )
 
     def sum_rows():
-        chain_products(slot_total, backward, chain, table, row_table)
+        chain_products(slot_total, backward, chain, table, ROW_BEFORE)
 
         def finish(index, carry):
-            rows[index] = (scale * chain[table[row_last + index]]).astype(jnp.bfloat16)
+            rows[index] = (scale * chain[table[ROW_LAST, index]]).astype(jnp.bfloat16)
             return carry
 
         lax.fori_loop(0, row_blocks, finish, 0)
@@ -434,7 +492,25 @@
 
     def tiles_of(offset, chunk, inner):
         first = wide.first(offset, chunk, inner)
-        make_tiles(table, right_table, left, right, tiles, first, wide.size, scale)
+        make_tiles(table, left, right, tiles, first, wide.size, scale)
+
+    def update(index, gradient):
+        slot = wide.me * owned + index
+        live = table[LIVE, slot] == 1
+        weight, first, second = new_weights[index], new_first[index], new_second[index]
+        mean = factor[0, slot] * first + (1.0 - beta_one) * gradient
+        square = factor[2, slot] * second + (1.0 - beta_two) * gradient * gradient
+        spread = jnp.sqrt(factor[3, slot] * square) + epsilon
+        base = jnp.where(table[FRESH, slot] == 1, 0.0, weight)
+        moved = (1.0 - learn_rate * decay_rate) * base
+        moved -= learn_rate * (factor[1, slot] * mean / spread)
+        new_weights[index] = jnp.where(live, moved, weight)
+        new_first[index] = jnp.where(live, mean, first)
+        new_second[index] = jnp.where(live, square, second)
+
+    def store_row(index, total):
+        at = pl.ds(pl.multiple_of(index * side, side), side)
+        rows_out[:, at] = total.astype(jnp.bfloat16)
 
     far_steps = [(o, k) for o in range(1, wide.outer) for k in range(wide.chunks)]
     last_far = len(far_steps) - 1
@@ -456,22 +532,27 @@
         high = (chunk + 1) * len(thin_pairs) // wide.chunks
         for pair in thin_pairs[low:high]:
             thin.send_pair(*pair)
+    for copy in moments:
+        copy.wait()
     for chunk in range(wide.chunks - 1):
-        wide.total(chunk)
+        wide.total(chunk, update)
     for chunk in range(thin.chunks):
-        thin.total(chunk)
-    wide.total(wide.chunks - 1)
+        thin.total(chunk, store_row)
     line.finish()
     wing.finish()
+    wide.total(wide.chunks - 1, update)
     wide.finish()
     thin.finish()
 
 
-def run_step(table, weights, tokens, grad_out, columns, row_blocks, scale):
+def run_step(
+    weights, first, second, tokens, grad_out, mask, regrown, last_step, step_now, scale
+):
     sizes = (lax.axis_size("dp"), lax.axis_size("tensor"))
     owned, side = weights.shape[0], weights.shape[1]
     tok_count = tokens.shape[0]
     local_rows = tokens.shape[1] // side
+    columns, row_blocks = mask.shape[1:]
     slot_total = owned * sizes[0]
     outer = [size // INNER for size in sizes]
     gather_chunks = (math.gcd(8, owned), math.gcd(4, 2 * local_rows))
@@ -479,6 +560,7 @@
     block = (tok_count, side)
     tile = (side, side)
     dma = pltpu.SemaphoreType.DMA
+    width = -(-max(slot_total, row_blocks, 2 * columns) // 128) * 128
 
     def scratch(count, shape, kind=jnp.bfloat16):
         return pltpu.VMEM((count,) + shape, kind)
@@ -486,7 +568,6 @@
     shapes = [
         scratch(slot_total, tile),
         scratch(2 * local_rows * sizes[1], block),
-        scratch(owned, tile, jnp.float32),
         scratch(slot_total + 1, block, jnp.float32),
         scratch(2 * columns, block),
         scratch(slot_total, tile),
@@ -495,8 +576,13 @@
         scratch(max(outer[0] - 1, 1) * owned, tile),
         scratch(outer[1] * local_rows, block),
         scratch(max(outer[1] - 1, 1) * local_rows, block),
+        pltpu.VMEM((8, width), jnp.int32),
+        pltpu.VMEM((8, width), jnp.float32),
+        pltpu.SMEM((8, width), jnp.int32),
+        pltpu.SMEM((8, width), jnp.float32),
         dma((2 * local_rows,)),
         dma((gather_chunks[0],)),
+        dma((4,)),
     ]
     for size, chunks in zip(sizes, gather_chunks):
         shapes += [dma((size * chunks,))] + [dma((size // INNER * chunks,))] * 3
@@ -507,22 +593,15 @@
     anywhere = pl.BlockSpec(memory_space=pl.ANY)
     return pl.pallas_call(
         functools.partial(step_kernel, sizes, gather_chunks, reduce_chunks, scale),
-        out_shape=(
-            jax.ShapeDtypeStruct((owned,) + tile, jnp.float32),
-            jax.ShapeDtypeStruct((local_rows,) + block, jnp.bfloat16),
-        ),
-        in_specs=[smem, anywhere, anywhere, anywhere],
-        out_specs=(vmem, vmem),
+        out_shape=(pltpu.VMEM(tokens.shape, jnp.bfloat16),)
+        + (pltpu.VMEM((owned,) + tile, jnp.float32),) * 3,
+        in_specs=[anywhere] * 5 + [vmem] * 3 + [smem],
+        out_specs=(vmem,) * 4,
         scratch_shapes=shapes,
         compiler_params=pltpu.CompilerParams(
-            collective_id=0, has_side_effects=True, vmem_limit_bytes=62 * 1024 * 1024
+            collective_id=0, has_side_effects=True, vmem_limit_bytes=49 * 1024 * 1024
         ),
-    )(table, weights, tokens, grad_out)
-
-
-def last_where(matches):
-    places = jnp.arange(1, matches.shape[1] + 1, dtype=jnp.int32)
-    return jnp.max(jnp.where(matches, places[None, :], 0), axis=1)
+    )(weights, first, second, tokens, grad_out, mask, regrown, last_step, step_now)
 
 
 def per_device(
@@ -537,65 +616,19 @@
     step_now,
 ):
     scale_factor = 3.0 / math.sqrt(D)
-    tok_count = tokens.shape[0]
-    owned_slots = packed_weight_blocks.shape[0]
-    block_size = packed_weight_blocks.shape[1]
-    row_blocks = block_mask.shape[1]
-    column_blocks = block_mask.shape[2]
-    local_rows = tokens.shape[1] // block_size
-    groups = lax.axis_size("dp")
-    slot_total = owned_slots * groups
-    step_value = step_now[0]
-    block_index, slot_regrown, slot_last, live_count, _ = slot_table(
-        block_mask, regrown, last_step, slot_total
-    )
-    matrix_of = block_index // (row_blocks * column_blocks)
-    row_of = block_index // column_blocks % row_blocks
-    column_of = block_index % column_blocks
-    slot_ids = jnp.arange(slot_total, dtype=jnp.int32)
-    usable = (slot_ids < live_count) & (slot_regrown == 0)
-    left_at = (row_of // local_rows * 2 + matrix_of) * local_rows + row_of % local_rows
-    right_at = matrix_of * column_blocks + column_of
-    column_key = jnp.where(usable, right_at, -1)
-    row_key = jnp.where(usable & (matrix_of == 0), row_of, -1)
-    earlier = slot_ids[None, :] < slot_ids[:, None]
-    table = jnp.concatenate(
-        [
-            left_at,
-            right_at,
-            last_where((right_at[:, None] == column_key[None, :]) & earlier),
-            last_where((row_of[:, None] == row_key[None, :]) & earlier),
-            last_where(jnp.arange(2 * column_blocks, dtype=jnp.int32)[:, None] == column_key),
-            last_where(jnp.arange(row_blocks, dtype=jnp.int32)[:, None] == row_key),
-        ]
-    )
-    block_grads, summed_rows = run_step(
-        table,
-        packed_weight_blocks,
-        tokens,
-        grad_out,
-        column_blocks,
-        row_blocks,
-        scale_factor,
-    )
-    input_grad = (
-        summed_rows.transpose(1, 0, 2).reshape(tok_count, tokens.shape[1]).astype(jnp.bfloat16)
-    )
-    owner_first = lax.axis_index("dp") * owned_slots
-    mine_regrown = lax.dynamic_slice_in_dim(slot_regrown, owner_first, owned_slots)
-    mine_last = lax.dynamic_slice_in_dim(slot_last, owner_first, owned_slots)
-    live_slots = owner_first + jnp.arange(owned_slots, dtype=jnp.int32) < live_count
-    new_weights, new_first, new_second = adam_step(
+    mask, fresh, last = (grid.transpose(0, 2, 1) for grid in (block_mask, regrown, last_step))
+    return run_step(
         packed_weight_blocks,
         packed_first_moments,
         packed_second_moments,
-        block_grads,
-        live_slots,
-        mine_regrown,
-        mine_last,
-        step_value,
-    )
-    return (input_grad, new_weights, new_first, new_second)
+        tokens,
+        grad_out,
+        mask,
+        fresh,
+        last,
+        step_now,
+        scale_factor,
+    )
 
 
 def solution(mesh):

time: 136 us -> 122 us (0.90)
  other arithmetic: 16.3 us -> 0 us
  local copies, waits for them, and re-layouts: 3.01 us -> 6.74 us
    select_n x5 -> x0, other arithmetic: 13 us -> none  [the longest x1 11.6 us: adam_step(): jnp.where(keep_slot, new_second, second_in)]
    unnamed x1 -> x4, local copies, waits for them, and re-layouts: 0.85 us -> 6.74 us
where the time goes in v2:
time: 122 us
  Pallas kernels  114 us (93%)
  local copies, waits for them, and re-layouts  6.74 us (6%)
  between operations  1.29 us (1%)
    pallas_call x1, Pallas kernels, run_step(): pl.pallas_call(functools.partial(step_kernel, sizes, gather_chunks, reduc...  114 us
    unnamed x4, local copies, waits for them, and re-layouts  6.74 us

profile of v2, /device:TPU:0, one launch (start us, length us, event | category | flops | bytes accessed | tf_op | source)
XLA Modules:
  0.0 122.0 jit_solution(1982074622641361390)
XLA Ops:
  1.3 114.0 %shard_map.120 = (bf16[128,1024]{1,0:T(8,128)(2,1)S(1)}, f32[64,128,128]{2,1,0:T(8,128)S(1)}, f32[64,128,128]{2,1,0:T(8,128)S(1)}, f32[64,128,128]{2,1,0:T(8,128)S(1)}) custom-call(f32[64,128,128]{2,1,0:T(8,128)} %weights.1, f32[64,128,128]{2,1,0:T(8,128)} %first_in.1, f32[64,128,128]{2,1,0:T(8,128)} %second_in.1, bf16[128,1024]{1,0:T(8,128)(2,1)} %tokens.1, ...), custom_call_target="tpu_custom_call" | custom-call | tf_op jit(solution)/shard_map/pallas_call | solution.py:594
  115.3 0.7 copy.17
  116.0 2.0 %copy.18 = f32[64,128,128]{2,1,0:T(8,128)} copy(f32[64,128,128]{2,1,0:T(8,128)S(1)} %get-tuple-element.5) | data formatting | bytes 8388608
  118.0 2.0 %copy.19 = f32[64,128,128]{2,1,0:T(8,128)} copy(f32[64,128,128]{2,1,0:T(8,128)S(1)} %get-tuple-element.6) | data formatting | bytes 8388608
  120.0 2.0 %copy.20 = f32[64,128,128]{2,1,0:T(8,128)} copy(f32[64,128,128]{2,1,0:T(8,128)S(1)} %get-tuple-element.7) | data formatting | bytes 8388608

commit v3 on v2

--- a/solution.py
+++ b/solution.py
@@ -27,7 +27,9 @@
     return jnp.max(jnp.where(matches, places, 0), axis=0, keepdims=True)
 
 
-def build_tables(mask, regrown, last_step, step_now, places, factors, sources, local_rows):
+def build_tables(
+    mask, regrown, last_step, step_now, places, factors, sources, local_rows, order
+):
     columns, rows = mask.shape[1:]
     width = places.shape[1]
     right_bits = (2 * columns - 1).bit_length()
@@ -77,18 +79,18 @@
     usable = (live_down == 1) & (fresh_down == 0)
     column_key = jnp.where(usable, right_down, -1)
     row_key = jnp.where(usable & (right_down < columns), left_down, -1)
-    down = lax.broadcasted_iota(jnp.int32, (width, width), 0)
-    across = lax.broadcasted_iota(jnp.int32, (width, width), 1)
-    place = down + 1
-    earlier = down < across
+    down = lax.broadcasted_iota(jnp.int32, (width, 1), 0)
+    across = lax.broadcasted_iota(jnp.int32, (1, width), 1)
+    earlier = order(down) < order(across)
+    place = order(down) + 1
     lane = lax.broadcasted_iota(jnp.int32, (1, width), 1)
     lane_left = lane + row_source(lane) * local_rows
     places[0:1, :] = left
     places[1:2, :] = right
     places[2:3, :] = last_place((column_key == right) & earlier, place)
-    places[3:4, :] = last_place((row_key == left) & earlier, place)
+    places[3:4, :] = last_place((row_key == left) & (down < across), down + 1)
     places[4:5, :] = last_place(column_key == lane, place)
-    places[5:6, :] = last_place(row_key == lane_left, place)
+    places[5:6, :] = last_place(row_key == lane_left, down + 1)
     places[6:7, :] = live
     places[7:8, :] = fresh
     step = step_now[0]
@@ -134,9 +136,10 @@
 
 
 class LineGather:
-    def __init__(self, axis, size, chunks, shard, out, sems):
+    def __init__(self, axis, size, chunks, shard, out, sems, balanced=False):
         self.axis, self.chunks, self.out = axis, chunks, out
-        self.recv, self.up, self.down, self.across = sems
+        self.recv, self.up, self.down, self.across, self.pass_up, self.pass_down = sems
+        self.balanced = balanced
         self.outer = size // INNER
         me = lax.axis_index(axis)
         self.me, self.mine, self.inner = me, me // INNER, me % INNER
@@ -151,6 +154,8 @@
             "up": (self.up, self.me + INNER),
             "down": (self.down, self.me - INNER),
             "across": (self.across, self.mine * INNER + 1 - self.inner),
+            "pass_up": (self.pass_up, self.me + INNER),
+            "pass_down": (self.pass_down, self.me - INNER),
         }[way]
         recv = self.recv.at[index * self.chunks + chunk]
         return remote(at, at, sem.at[slot], recv, self.axis, target)
@@ -171,8 +176,24 @@
 
         self.copy(mine, chunk, "across").start()
 
+    def passed(self, chunk):
+        return self.balanced and chunk % 2 == 1
+
+    def pass_on(self, chunk):
+        other = 1 - self.inner
+        self.wait_recv(self.mine, chunk, other)
+
+        @pl.when(self.mine + 1 < self.outer)
+        def _():
+            self.copy(self.mine, chunk, "pass_up", other).start()
+
+        @pl.when(self.mine > 0)
+        def _():
+            self.copy(self.mine, chunk, "pass_down", other).start()
+
     def step(self, distance, chunk):
         low, high = self.mine - distance, self.mine + distance
+        crosses = distance > 1 or not self.passed(chunk)
 
         @pl.when(low >= 0)
         def _():
@@ -182,7 +203,8 @@
             def _():
                 self.copy(low, chunk, "up").start()
 
-            self.copy(low, chunk, "across").start()
+            if crosses:
+                self.copy(low, chunk, "across").start()
 
         @pl.when(high < self.outer)
         def _():
@@ -192,16 +214,39 @@
             def _():
                 self.copy(high, chunk, "down").start()
 
-            self.copy(high, chunk, "across").start()
+            if crosses:
+                self.copy(high, chunk, "across").start()
 
     def arrive(self, source):
         for chunk in range(self.chunks):
-            self.wait_recv(source, chunk, 1 - self.inner)
+            if self.passed(chunk):
+
+                @pl.when(self.mine != source)
+                def _(chunk=chunk):
+                    self.wait_recv(source, chunk, 1 - self.inner)
+
+            else:
+                self.wait_recv(source, chunk, 1 - self.inner)
 
     def finish(self):
         for source in range(self.outer):
             for chunk in range(self.chunks):
-                self.copy(source, chunk, "across").wait_send()
+                if self.passed(chunk):
+
+                    @pl.when((self.mine != source + 1) & (self.mine + 1 != source))
+                    def _(source=source, chunk=chunk):
+                        self.copy(source, chunk, "across").wait_send()
+
+                    @pl.when((self.mine == source) & (self.mine + 1 < self.outer))
+                    def _(source=source, chunk=chunk):
+                        self.copy(source, chunk, "pass_up", 1 - self.inner).wait_send()
+
+                    @pl.when((self.mine == source) & (self.mine > 0))
+                    def _(source=source, chunk=chunk):
+                        self.copy(source, chunk, "pass_down", 1 - self.inner).wait_send()
+
+                else:
+                    self.copy(source, chunk, "across").wait_send()
 
                 @pl.when((self.mine >= source) & (self.mine + 1 < self.outer))
                 def _(source=source, chunk=chunk):
@@ -301,14 +346,15 @@
                     self.far_copy(offset, chunk).wait_send()
 
 
-def chain_products(count, product, chain, table, previous):
+def chain_products(count, product, chain, table, previous, slot, place):
     unroll = math.gcd(UNROLL, count)
 
     def step(index, carry):
         base = index * unroll
-        parts = [product(base + k) for k in range(unroll)]
+        parts = [product(slot + base + k) for k in range(unroll)]
         for k in range(unroll):
-            chain[base + k + 1] = parts[k] + chain[table[previous, base + k]]
+            before = table[previous, slot + base + k]
+            chain[place + base + k + 1] = parts[k] + chain[before]
         return carry
 
     lax.fori_loop(0, count // unroll, step, 0)
@@ -370,13 +416,15 @@
     owned, side = new_weights.shape[0], new_weights.shape[1]
     slot_total, columns, row_blocks = packed.shape[0], right.shape[0] // 2, rows.shape[0]
     local_rows = rows_out.shape[1] // side
-    line = LineGather("dp", sizes[0], gather_chunks[0], owned, packed, sems[:4])
-    wing = LineGather("tensor", sizes[1], gather_chunks[1], 2 * local_rows, left, sems[4:8])
+    line = LineGather("dp", sizes[0], gather_chunks[0], owned, packed, sems[:6])
+    wing = LineGather(
+        "tensor", sizes[1], gather_chunks[1], 2 * local_rows, left, sems[6:12], True
+    )
     wide = PairReduce(
-        "dp", sizes[0], reduce_chunks[0], tiles, owned, wide_near, wide_far, sems[8:12]
+        "dp", sizes[0], reduce_chunks[0], tiles, owned, wide_near, wide_far, sems[12:16]
     )
     thin = PairReduce(
-        "tensor", sizes[1], reduce_chunks[1], rows, local_rows, thin_near, thin_far, sems[12:]
+        "tensor", sizes[1], reduce_chunks[1], rows, local_rows, thin_near, thin_far, sems[16:]
     )
 
     def load_left(index):
@@ -432,34 +480,79 @@
     for copy in moments:
         copy.start()
     chain[0] = jnp.zeros(chain.shape[1:], jnp.float32)
+    size = owned // line.chunks
+
+    def pair_at(offset):
+        return lax.rem(line.mine + offset, line.outer)
+
+    staged = line.outer == 2
+    segments = []
+    for offset in range(line.outer):
+        first = pair_at(offset) * INNER * owned
+        if offset == 0 or not staged:
+            segments.append((offset, None, first, INNER * owned))
+        else:
+            for chunk in range(line.chunks):
+                for inner in range(INNER):
+                    at = first + inner * owned + chunk * size
+                    segments.append((offset, chunk if inner == 0 else None, at, size))
+
+    def order(slots):
+        ordered, place = slots, 0
+        for _, _, first, count in segments:
+            inside = (slots >= first) & (slots < first + count)
+            ordered = jnp.where(inside, slots - first + place, ordered)
+            place += count
+        return ordered
+
     build_tables(
-        mask, regrown, last_step, step_now, places, factors, sizes[1], local_rows
+        mask, regrown, last_step, step_now, places, factors, sizes[1], local_rows, order
     )
     for copy in load_tables:
         copy.start()
 
     events = []
-    for gather, weight in ((line, 1.5), (wing, 1.0)):
+    for gather, weight in ((line, 1.2), (wing, 1.0)):
         for chunk in range(gather.chunks):
             for distance in range(1, gather.outer):
                 passed = (distance - 1 + (chunk + 1) / gather.chunks) / (gather.outer - 1)
-                events.append((weight * passed, gather, distance, chunk))
+                events.append((weight * passed, gather.step, (distance, chunk), gather is line))
+            if gather.passed(chunk):
+                passed = (chunk + 1) / gather.chunks / (gather.outer - 1)
+                events.append((weight * passed, gather.pass_on, (chunk,), False))
     events.sort(key=lambda event: event[0])
-    for _, gather, distance, chunk in events:
-        gather.step(distance, chunk)
+    deferred = []
+    for when, act, which, late in events:
+        if late and when > 1.0:
+            deferred.append((act, which))
+        else:
+            act(*which)
     for copy in load_tables:
         copy.wait()
     for source in range(wing.outer):
         wing.arrive(source)
-    for source in range(line.outer):
-        line.arrive(source)
 
     def forward(slot):
         return jnp.dot(
             left[table[LEFT, slot]], packed[slot], preferred_element_type=jnp.float32
         )
 
-    chain_products(slot_total, forward, chain, table, COLUMN_BEFORE)
+    if not staged:
+        for act, which in deferred:
+            act(*which)
+        for offset in range(1, line.outer):
+            line.arrive(pair_at(offset))
+        deferred = []
+    line.arrive(line.mine)
+    place = 0
+    for offset, chunk, first, count in segments:
+        if chunk is not None:
+            if deferred and deferred[0][1] == (offset, chunk):
+                act, which = deferred.pop(0)
+                act(*which)
+            line.wait_recv(pair_at(offset), chunk, 1 - line.inner)
+        chain_products(count, forward, chain, table, COLUMN_BEFORE, first, place)
+        place += count
 
     def activate(column, carry):
         pre_act = scale * chain[table[COLUMN_LAST, column]]
@@ -479,7 +572,7 @@
         )
 
     def sum_rows():
-        chain_products(slot_total, backward, chain, table, ROW_BEFORE)
+        chain_products(slot_total, backward, chain, table, ROW_BEFORE, 0, 0)
 
         def finish(index, carry):
             rows[index] = (scale * chain[table[ROW_LAST, index]]).astype(jnp.bfloat16)
@@ -585,7 +678,7 @@
         dma((4,)),
     ]
     for size, chunks in zip(sizes, gather_chunks):
-        shapes += [dma((size * chunks,))] + [dma((size // INNER * chunks,))] * 3
+        shapes += [dma((size * chunks,))] + [dma((size // INNER * chunks,))] * 5
     for count, chunks in zip(outer, reduce_chunks):
         shapes += [dma((count * chunks,))] * 2 + [dma((max(count - 1, 1) * chunks,))] * 2
     vmem = pl.BlockSpec(memory_space=pltpu.VMEM)
@@ -604,6 +697,29 @@
     )(weights, first, second, tokens, grad_out, mask, regrown, last_step, step_now)
 
 
+def copy_out(*refs):
+    count = len(refs) // 2
+    copies = [
+        pltpu.make_async_copy(refs[at], refs[count + at], refs[-1].at[at])
+        for at in range(count)
+    ]
+    for copy in copies:
+        copy.start()
+    for copy in copies:
+        copy.wait()
+
+
+def write_out(*arrays):
+    return pl.pallas_call(
+        copy_out,
+        out_shape=tuple(jax.ShapeDtypeStruct(x.shape, x.dtype) for x in arrays),
+        in_specs=[pl.BlockSpec(memory_space=pltpu.VMEM)] * len(arrays),
+        out_specs=(pl.BlockSpec(memory_space=pl.ANY),) * len(arrays),
+        scratch_shapes=[pltpu.SemaphoreType.DMA((len(arrays),))],
+        compiler_params=pltpu.CompilerParams(vmem_limit_bytes=14 * 1024 * 1024),
+    )(*arrays)
+
+
 def per_device(
     tokens,
     grad_out,
@@ -617,7 +733,7 @@
 ):
     scale_factor = 3.0 / math.sqrt(D)
     mask, fresh, last = (grid.transpose(0, 2, 1) for grid in (block_mask, regrown, last_step))
-    return run_step(
+    results = run_step(
         packed_weight_blocks,
         packed_first_moments,
         packed_second_moments,
@@ -629,6 +745,7 @@
         step_now,
         scale_factor,
     )
+    return write_out(*results)
 
 
 def solution(mesh):

time: 122 us -> 120 us (0.984)
  local copies, waits for them, and re-layouts: 6.74 us -> 0 us
  Pallas kernels: 114 us -> 119 us
    unnamed x4 -> x0, local copies, waits for them, and re-layouts: 6.74 us -> none
    pallas_call x0 -> x1, Pallas kernels: none -> 4.78 us  [write_out(): pl.pallas_call(copy_out, out_shape=tuple((jax.ShapeDtypeStruct(x.shape, x...]
where the time goes in v3:
time: 120 us
  Pallas kernels  119 us (99%)
  between operations  1.29 us (1%)
    pallas_call x1, Pallas kernels, run_step(): pl.pallas_call(functools.partial(step_kernel, sizes, gather_chunks, reduc...  114 us
    pallas_call x1, Pallas kernels, write_out(): pl.pallas_call(copy_out, out_shape=tuple((jax.ShapeDtypeStruct(x.shape, x...  4.78 us

profile of v3, /device:TPU:0, one launch (start us, length us, event | category | flops | bytes accessed | tf_op | source)
XLA Modules:
  0.0 119.8 jit_solution(9972107931047145189)
XLA Ops:
  1.3 113.7 %shard_map.120 = (bf16[128,1024]{1,0:T(8,128)(2,1)S(1)}, f32[64,128,128]{2,1,0:T(8,128)S(1)}, f32[64,128,128]{2,1,0:T(8,128)S(1)}, f32[64,128,128]{2,1,0:T(8,128)S(1)}) custom-call(f32[64,128,128]{2,1,0:T(8,128)} %weights.1, f32[64,128,128]{2,1,0:T(8,128)} %first_in.1, f32[64,128,128]{2,1,0:T(8,128)} %second_in.1, bf16[128,1024]{1,0:T(8,128)(2,1)} %tokens.1, ...), custom_call_target="tpu_custom_call" | custom-call | tf_op jit(solution)/shard_map/pallas_call | solution.py:687
  115.0 4.8 %shard_map.121 = (bf16[128,1024]{1,0:T(8,128)(2,1)}, f32[64,128,128]{2,1,0:T(8,128)}, f32[64,128,128]{2,1,0:T(8,128)}, f32[64,128,128]{2,1,0:T(8,128)}) custom-call(bf16[128,1024]{1,0:T(8,128)(2,1)S(1)} %get-tuple-element.8.refs_0_, f32[64,128,128]{2,1,0:T(8,128)S(1)} %get-tuple-element.9.refs_1_, f32[64,128,128]{2,1,0:T(8,128)S(1)} %get-tuple-element.10.refs_2_, ...), custom_call_target="tpu_custom_call" | custom-call | tf_op jit(solution)/shard_map/pallas_call | solution.py:713
